TPU v7x, 128 devices: a whole 4x4x4 slice. The times are simulated.
128 devices in a mesh: lat: 8 (over z, core), lon: 16 (over x, y).
Axes of the slice: x: 4, y: 4, z: 4, core: 2. Of those that a mesh axis runs over, the one named last changes fastest.
Arguments:
- control: float32 [32, 1024, 512], P('lat', 'lon'), may hold values from -1.2 to 1.2
- vert_factor: float32 [4, 128, 128], replicated, may hold values from -0.5 to 0.5
- zonal_factor: float32 [1024, 1024], replicated, may hold values from -0.1875 to 0.1875
- obs_dest: int32 [98304, 1], P(('lat', 'lon')), may hold values from 0 to 127; in each aligned block of 768 rows (0 to 767, 768 to 1535, ...) at most 9 rows name the same one
- obs_cell: int32 [98304], P(('lat', 'lon')), may hold values from 0 to 255
- obs_offset: int32 [98304], P(('lat', 'lon')), may hold values from 0 to 96
- obs_count: int32 [128], P(('lat', 'lon')), may hold values from 384 to 768, as said below
- departure: float32 [98304], P(('lat', 'lon')), may hold values from -6 to 6
- obs_rinv: float32 [98304], P(('lat', 'lon')), may hold values from 0.25 to 4
- obs_weights: float32 [98304, 128], P(('lat', 'lon')), may hold values from 0 to 1
Outputs:
- gradient: float32 [32, 1024, 512], P('lat', 'lon')
Inputs may be any that keep to these rules, and one draw needn't show every extreme that they name: Among the 768 observations of one device, at most 9 have the same obs_dest, and some value is taken exactly 9 times on some devices. `obs_count`: some device holds exactly 768 live observations.
All inputs are finite; a program needn't handle non-finite values.
Results may differ from a plain program's by a relative error of at most 0.000068.
Values sent between devices are 32-bit elements; how exact they have to be, the bound alone decides.
A program may use at most 64 MiB of HBM per device.

v0:
```python
import jax
import jax.numpy as jnp
from jax import lax
from jax.sharding import PartitionSpec as P

F = 4
LEV = 128
KW = 32


def place_levels(blocks, offsets):
    level_ids = jnp.arange(LEV, dtype=jnp.int32)
    block_ids = jnp.arange(KW, dtype=jnp.int32)
    shift_mat = (
        level_ids[None, None, :] - offsets[:, None, None] == block_ids[None, :, None]
    ).astype(jnp.float32)
    placed = jnp.einsum("rfk,rkl->rfl", blocks, shift_mat, precision=lax.Precision.HIGHEST)
    return placed.reshape(blocks.shape[0], F * LEV)


def per_device(
    control,
    vert_factor,
    zonal_factor,
    obs_dest,
    obs_cell,
    obs_offset,
    obs_count,
    departure,
    obs_rinv,
    obs_weights,
):
    lat_count = lax.axis_size("lat")
    lon_count = lax.axis_size("lon")
    devices = lat_count * lon_count
    n_obs = obs_cell.shape[0]
    capacity = max(2, 3 * n_obs // (2 * devices))
    slots = devices * capacity
    lat_rows = control.shape[0]
    lon_cols = control.shape[1]
    depth = control.shape[2]
    columns = lat_rows * lon_cols
    positions = jnp.arange(n_obs, dtype=jnp.int32)
    live = positions < obs_count[0]
    scaled = jnp.where(live, obs_rinv * departure, jnp.float32(0.0))
    values = obs_weights * scaled[:, None]
    target = obs_dest[:, 0]
    onehot = (target[:, None] == jnp.arange(devices, dtype=jnp.int32)[None, :]).astype(jnp.int32)
    ranks = jnp.sum(jnp.cumsum(onehot, axis=0) * onehot, axis=1) - 1
    slot_of = target * capacity + ranks
    slot_hit = slot_of[None, :] == jnp.arange(slots, dtype=jnp.int32)[:, None]
    slot_mat = slot_hit.astype(jnp.float32)
    cell_label = jnp.sum(jnp.where(slot_hit, obs_cell[None, :], 0), axis=1)
    profile = place_levels(values.reshape(n_obs, F, KW), obs_offset)
    payload = jnp.dot(slot_mat, profile, precision=lax.Precision.HIGHEST)
    labels = cell_label[:, None]
    width = payload.shape[1]
    label_width = labels.shape[1]
    got, got_labels = (
        lax.all_to_all(
            payload.reshape(devices, capacity, width),
            ("lat", "lon"),
            split_axis=0,
            concat_axis=0,
            tiled=True,
        ),
        lax.all_to_all(
            labels.reshape(devices, capacity, label_width),
            ("lat", "lon"),
            split_axis=0,
            concat_axis=0,
            tiled=True,
        ),
    )
    got = got.reshape(slots, width)
    got_labels = got_labels.reshape(slots, label_width)
    cell_mat = (jnp.arange(columns, dtype=jnp.int32)[:, None] == got_labels[:, 0][None, :]).astype(
        jnp.float32
    )
    adjoint = jnp.dot(cell_mat, got, precision=lax.Precision.HIGHEST)
    blocks = adjoint.reshape(lat_rows, lon_cols, F, LEV)
    vertical = jnp.einsum("abfk,fkl->aflb", blocks, vert_factor, precision=lax.Precision.HIGHEST)
    vertical = vertical.reshape(lat_rows, depth, lon_cols)
    product = jnp.einsum(
        "alm,mn->aln",
        lax.all_to_all(vertical, "lon", split_axis=1, concat_axis=2, tiled=True),
        zonal_factor,
        precision=lax.Precision.HIGHEST,
    )
    zonal = lax.all_to_all(product, "lon", split_axis=2, concat_axis=1, tiled=True)
    return control + jnp.transpose(zonal, (0, 2, 1))


def solution(mesh):
    return jax.shard_map(
        per_device,
        mesh=mesh,
        in_specs=(
            P("lat", "lon", None),
            P(),
            P(),
            P(("lat", "lon"), None),
            P(("lat", "lon")),
            P(("lat", "lon")),
            P(("lat", "lon")),
            P(("lat", "lon")),
            P(("lat", "lon")),
            P(("lat", "lon"), None),
        ),
        out_specs=P("lat", "lon", None),
        check_vma=False,
    )
```

profile of v0, /device:TPU:1, one launch (start us, length us, event | category | flops | bytes accessed | tf_op | source)
XLA Modules:
  0.0 144.3 jit_solution(14904634939275345926)
XLA Ops:
  0.0 0.0 copy-start
  0.0 0.0 copy-start.5
  0.0 0.0 copy-start.1
  0.0 0.0 copy-start.4
  0.0 0.0 copy-start.3
  0.0 0.8 reduce
  0.8 0.1 copy.54
  0.9 0.2 fusion.13
  1.2 0.0 copy-start.2
  1.2 0.1 copy.55
  1.3 0.3 fusion.15
  1.6 0.0 copy-done.5
  1.6 0.4 select_reduce_fusion
  2.0 0.8 reshape_broadcast_in_dim.3
  2.9 11.5 %all-to-all-start = ((s32[128,9,1]{1,2,0:T(1,128)}), s32[128,9,1]{1,2,0:T(1,128)S(1)}, u32[]{:S(2)}, u32[]{:S(2)}) async-start(s32[128,9,1]{1,2,0:T(1,128)} %bitcast.3), calls=%async_computation | async-start | bytes 131072 | tf_op jit(solution)/shard_map/all_to_all | solution.py:67
  14.4 0.0 copy-done.1
  14.4 0.2 copy.57
  15.2 0.0 copy-done.4
  15.2 0.0 copy-done.3
  15.3 0.7 copy.58
  16.0 0.0 copy-done.2
  16.0 0.2 iota_subtract_fusion
  16.2 6.1 %fusion = f32[768,4,128]{2,1,0:T(4,128)S(1)} fusion(f32[768,4,32]{2,1,0:T(4,128)S(1)} %copy.58, s32[768,128]{1,0:T(8,128)S(1)} %iota_subtract_fusion), kind=kOutput, calls=%fused_computation.1 | convolution fusion | flops 154140672 | bytes 2359296 | tf_op jit(solution)/shard_map/rfk,rkl->rfl/dot_general | solution.py:17
  22.3 0.6 reshape.105
  22.9 3.2 %fusion.4 = f32[128,9,512]{2,0,1:T(8,128)S(1)} fusion(f32[768,512,1]{1,0,2:T(8,128)S(1)} %reshape.105, s32[128,9]{0,1:T(8,128)S(1)} %multiply_add_fusion, s32[768]{0:T(1024)S(1)} %add_add_fusion), kind=kOutput, calls=%fused_computation.7 | convolution fusion | flops 5436702720 | bytes 3939840 | tf_op jit(solution)/shard_map/dot_general | solution.py:55
  26.1 3.5 %copy.59 = f32[128,9,512]{2,1,0:T(8,128)} copy(f32[128,9,512]{2,0,1:T(8,128)S(1)} %fusion.4) | data formatting | bytes 4718592 | tf_op jit(solution)/shard_map/dot_general | solution.py:55
  29.6 0.0 all-to-all-done
  29.6 10.2 %all-to-all-start.1 = ((f32[128,9,512]{2,1,0:T(8,128)}), f32[128,9,512]{2,1,0:T(8,128)}, u32[]{:S(2)}, u32[]{:S(2)}) async-start(f32[128,9,512]{2,1,0:T(8,128)} %copy.59), calls=%async_computation.1 | async-start | bytes 8388608 | tf_op jit(solution)/shard_map/all_to_all | solution.py:60
  39.8 0.5 broadcast.87
  40.3 0.8 reduce.5
  41.1 0.2 eq.106
  41.3 50.8 %all-to-all-done.1 = f32[128,9,512]{2,1,0:T(8,128)} async-done(((f32[128,9,512]{2,1,0:T(8,128)}), f32[128,9,512]{2,1,0:T(8,128)}, u32[]{:S(2)}, u32[]{:S(2)}) %all-to-all-start.1) | async-done | bytes 2359328 | tf_op jit(solution)/shard_map/all_to_all | solution.py:60
  92.1 3.0 %reshape.103 = f32[1152,512]{1,0:T(8,128)S(1)} reshape(f32[128,9,512]{2,1,0:T(8,128)} %all-to-all-done.1) | data formatting | bytes 4718592 | tf_op jit(solution)/shard_map/reshape | solution.py:75
  95.1 2.0 %copy.60 = f32[512,1152]{1,0:T(8,128)} copy(f32[512,1152]{0,1:T(8,128)S(1)} %bitcast.55) | data formatting | bytes 4718592 | tf_op jit(solution)/shard_map/dot_general | solution.py:80
  97.1 3.1 %fusion.8 = f32[4,64,4,128]{3,1,0,2:T(8,128)S(1)} fusion(f32[4,128,1152,1]{2,1,3,0:T(8,128)} %bitcast.56, s32[1152]{0:T(1024)S(1)} %eq.106, s32[4,64]{1,0:T(4,128)S(1)} %multiply_add_fusion.1), kind=kOutput, calls=%fused_computation.12 | convolution fusion | flops 1812234240 | bytes 2889216 | tf_op jit(solution)/shard_map/dot_general | solution.py:80
  100.2 0.0 copy-done
  100.2 0.6 convolution_bitcast_fusion
  100.9 0.4 copy.70
  101.3 1.0 reshape.122
  102.2 11.9 %all_to_all.46 = f32[16,1,8192]{2,1,0:T(1,128)S(1)} all-to-all(f32[16,1,8192]{2,1,0:T(1,128)S(1)} %reshape.122), channel_id=1, replica_groups=mesh['lat'=8,'lon'=16] {'lon'}, dimensions={0} | all-to-all | bytes 1048576 | tf_op jit(solution)/shard_map/all_to_all | solution.py:86
  114.1 0.5 broadcast.88
  114.7 1.9 %reduce.6 = f32[16,8192]{1,0:T(8,128)S(1)} reduce(f32[16,1,8192]{2,1,0:T(1,128)S(1)} %all_to_all.46, f32[]{:T(128)} %broadcast.88), dimensions={1}, to_apply=%all_to_all.34.reduce_sub_computation | reduce | bytes 1048580 | tf_op jit(solution)/shard_map/all_to_all | solution.py:86
  116.5 0.7 reshape.123
  117.2 0.1 copy.63
  117.3 0.6 copy.64
  117.9 0.3 all_to_all.37
  118.3 4.6 %fusion.2 = f32[4,32,1024]{2,1,0:T(8,128)S(1)} fusion(f32[4,32,1024]{2,1,0:T(8,128)S(1)} %all_to_all.37, f32[1024,1024]{1,0:T(8,128)} %param.12), kind=kOutput, calls=%fused_computation.3 | convolution fusion | flops 1610612736 | bytes 5242880 | tf_op jit(solution)/shard_map/alm,mn->aln/dot_general | solution.py:84
  122.8 0.9 copy.65
  123.7 1.4 reshape.124
  125.1 13.2 %all_to_all.47 = f32[16,1,8192]{2,1,0:T(1,128)S(1)} all-to-all(f32[16,1,8192]{2,1,0:T(1,128)S(1)} %reshape.124), channel_id=1, replica_groups=mesh['lat'=8,'lon'=16] {'lon'}, dimensions={0} | all-to-all | bytes 1048576 | tf_op jit(solution)/shard_map/all_to_all | solution.py:90
  138.3 1.9 %reduce.7 = f32[16,8192]{1,0:T(8,128)S(1)} reduce(f32[16,1,8192]{2,1,0:T(1,128)S(1)} %all_to_all.47, f32[]{:T(128)} %broadcast.88), dimensions={1}, to_apply=%all_to_all.38.reduce_sub_computation | reduce | bytes 1048580 | tf_op jit(solution)/shard_map/all_to_all | solution.py:90
  140.2 1.1 reshape.125
  141.2 0.8 copy.66
  142.1 0.3 copy.67
  142.4 1.9 %bitcast_add_fusion = f32[4,64,512]{2,1,0:T(8,128)} fusion(f32[4,64,512]{2,1,0:T(8,128)} %param.10, f32[4,512,64]{1,2,0:T(8,128)S(1)} %copy.67), kind=kLoop, calls=%fused_computation.17 | loop fusion | flops 131072 | bytes 1572864 | tf_op jit(solution)/shard_map/add | solution.py:91
  (8 shorter events, 0.1 us)
Async XLA Ops:
  0.0 100.2 %copy-start = (f32[4,128,128]{2,1,0:T(8,128)S(1)}, f32[4,128,128]{2,1,0:T(8,128)}, u32[]{:S(2)}) copy-start(f32[4,128,128]{2,1,0:T(8,128)} %param.11) | copy-start | bytes 786436
  0.0 1.6 %copy-start.5 = (s32[768]{0:T(1024)S(1)}, s32[768]{0:T(1024)}, u32[]{:S(2)}) copy-start(s32[768]{0:T(1024)} %param.14) | copy-start | bytes 9220
  0.0 14.4 %copy-start.1 = (f32[768,128]{1,0:T(8,128)S(1)}, f32[768,128]{1,0:T(8,128)}, u32[]{:S(2)}) copy-start(f32[768,128]{1,0:T(8,128)} %param.19) | copy-start | bytes 1179652
  0.0 15.2 %copy-start.4 = (f32[768]{0:T(1024)S(1)}, f32[768]{0:T(1024)}, u32[]{:S(2)}) copy-start(f32[768]{0:T(1024)} %param.17) | copy-start | bytes 9220
  0.0 15.2 %copy-start.3 = (f32[768]{0:T(1024)S(1)}, f32[768]{0:T(1024)}, u32[]{:S(2)}) copy-start(f32[768]{0:T(1024)} %param.18) | copy-start | bytes 9220
  1.2 14.8 %copy-start.2 = (s32[768]{0:T(1024)S(1)}, s32[768]{0:T(1024)}, u32[]{:S(2)}) copy-start(s32[768]{0:T(1024)} %param.15) | copy-start | bytes 9220
  2.9 26.7 %all-to-all-start = ((s32[128,9,1]{1,2,0:T(1,128)}), s32[128,9,1]{1,2,0:T(1,128)S(1)}, u32[]{:S(2)}, u32[]{:S(2)}) async-start(s32[128,9,1]{1,2,0:T(1,128)} %bitcast.3), calls=%async_computation | async-start | bytes 131072 | tf_op jit(solution)/shard_map/all_to_all | solution.py:67
  29.6 62.5 %all-to-all-start.1 = ((f32[128,9,512]{2,1,0:T(8,128)}), f32[128,9,512]{2,1,0:T(8,128)}, u32[]{:S(2)}, u32[]{:S(2)}) async-start(f32[128,9,512]{2,1,0:T(8,128)} %copy.59), calls=%async_computation.1 | async-start | bytes 8388608 | tf_op jit(solution)/shard_map/all_to_all | solution.py:60
where the time goes:
time: 147 us; the launch traced here: 144 us
  waiting for transfers between devices  50.8 us (35%)
  blocking collectives  25.1 us (17%)
  starting transfers between devices  21.7 us (15%)
  local copies, waits for them, and re-layouts  19.7 us (13%)
  matrix products  17.6 us (12%)
  other arithmetic  8.46 us (6%)
    all_to_all x1, waiting for transfers between devices, per_device(): lax.all_to_all(payload.reshape(devices, capacity, width), ('lat', 'lon'),...  50.8 us
    all_to_all x1, blocking collectives, per_device(): lax.all_to_all(product, 'lon', split_axis=2, concat_axis=1, tiled=True)  13.2 us
    all_to_all x1, blocking collectives, per_device(): lax.all_to_all(vertical, 'lon', split_axis=1, concat_axis=2, tiled=True)  11.9 us
    all_to_all x1, starting transfers between devices, per_device(): lax.all_to_all(labels.reshape(devices, capacity, label_width), ('lat', 'l...  11.5 us
    all_to_all x1, starting transfers between devices, per_device(): lax.all_to_all(payload.reshape(devices, capacity, width), ('lat', 'lon'),...  10.2 us
    dot_general x1, matrix products, place_levels(): jnp.einsum('rfk,rkl->rfl', blocks, shift_mat, precision=lax.Precision.HIG...  6.12 us
    dot_general x1, matrix products, per_device(): jnp.einsum('alm,mn->aln', lax.all_to_all(vertical, 'lon', split_axis=1, c...  4.58 us
    unnamed x17, local copies, waits for them, and re-layouts  4.28 us
  transfers between devices with their start and end apart: 2, of which 1 were waited for; matrix products, arithmetic and copies ran while one was open for 11% of the time, Pallas kernels for 0%

commit v1 on v0

v1 whole, which is shorter than its diff:
```python
import functools

import jax
import jax.numpy as jnp
from jax import lax
from jax.experimental import pallas as pl
from jax.experimental.pallas import tpu as pltpu
from jax.sharding import PartitionSpec as P

MESH = pl.DeviceIdType.MESH
F32, BF16, I32 = jnp.float32, jnp.bfloat16, jnp.int32
N_OBS = 768
CHUNKS = N_OBS // 128
SLOTS = 1152
MSG = 12
NT = (((1,), (1,)), ((), ()))


def ring(o):
    return min(o, 4 - o)


def offsets(everywhere):
    found = [
        (z, c, x, y)
        for z in range(4 if everywhere else 1)
        for c in range(2 if everywhere else 1)
        for x in range(4)
        for y in range(4)
        if (z, c, x, y) != (0, 0, 0, 0)
    ]
    return sorted(found, key=lambda o: -(ring(o[0]) + ring(o[2]) + ring(o[3])))


ALL = offsets(True)
BAND = offsets(False)


def peer(la, lo, o):
    z, c, x, y = o
    lat = (la // 2 + z) % 4 * 2 + (la % 2 + c) % 2
    lon = (lo // 4 + x) % 4 * 4 + (lo % 4 + y) % 4
    return lat, lon


def split(x):
    hi = x.astype(BF16)
    return hi, (x - hi.astype(F32)).astype(BF16)


def nt(a, b):
    return lax.dot_general(a, b, NT, preferred_element_type=F32)


def nn(a, b):
    return jnp.dot(a, b, preferred_element_type=F32)


def onehot(rows, index):
    ids = lax.broadcasted_iota(I32, (rows, 128), 0)
    return jnp.where(ids == index, 1.0, 0.0).astype(BF16)


def prepare(count_ref, dest_ref, cell_ref, off_ref, dep_ref, rinv_ref, w_ref, wt, lhs, pt, send):
    lane = lax.broadcasted_iota(I32, (1, 128), 1)
    rows = lax.broadcasted_iota(I32, (128, 128), 0)
    cols = lax.broadcasted_iota(I32, (128, 128), 1)
    before = jnp.concatenate(
        [jnp.where(rows < cols, 1.0, 0.0), jnp.ones((128, 128), F32)], axis=1
    ).astype(BF16)
    earlier = jnp.zeros((128, 128), F32)
    for c in range(CHUNKS):
        at = slice(128 * c, 128 * c + 128)
        dest, cell, off = dest_ref[:, at], cell_ref[:, at], off_ref[:, at]
        scaled = jnp.where(lane + 128 * c < count_ref[0], rinv_ref[:, at] * dep_ref[:, at], 0.0)
        wt[at, :] = w_ref[at, :].T * scaled
        mine = rows == dest
        counts = nn(jnp.where(mine, 1.0, 0.0).astype(BF16), before)
        rank = jnp.sum(jnp.where(mine, counts[:, :128] + earlier, 0.0), axis=0, keepdims=True)
        earlier = earlier + counts[:, 128:]
        rank = rank.astype(I32)
        slot = jnp.where(rank < 8, (dest >> 4) * 128 + rank * 16 + (dest & 15), 1024 + dest)
        pt[:, at] = onehot(SLOTS, slot)
        residue, turn = off & 3, off >> 2
        residue, turn = jnp.broadcast_to(residue, (8, 128)), jnp.broadcast_to(turn, (8, 128))
        shares = []
        for f in range(4):
            part = [wt[pl.ds(128 * c + 32 * f + k, 8, stride=4), :] for k in range(4)]
            for s in range(4):
                x = part[s]
                for e in range(1, 4):
                    x = jnp.where(residue == e, part[(s - e) % 4], x)
                by = turn + jnp.where(residue > s, 1, 0)
                for m in (1, 2, 4):
                    x = jnp.where((by & m) != 0, pltpu.roll(x, m, 0), x)
                shares.append(x)
        hi, lo = split(jnp.concatenate(shares, axis=0))
        lhs[0:128, at] = hi
        lhs[128:256, at] = lo
        ids = lax.broadcasted_iota(I32, (16, 128), 0)
        labels = jnp.where(ids == 0, cell, jnp.where(ids == 1, off, 0)).astype(F32)
        lhs[256:272, at] = labels.astype(BF16)

    for pair in range(4):
        got = nt(lhs[...], pt[256 * pair : 256 * pair + 256, :])
        value = got[0:128] + got[128:256]
        for half in range(2):
            a = 2 * pair + half
            at = slice(128 * half, 128 * half + 128)
            for j in range(16):
                send[pl.ds((a * 16 + j) * 16, 8), :] = value[8 * j : 8 * j + 8, at]
            send[pl.ds(a * 256 + 9, 16, stride=16), :] = jnp.broadcast_to(got[256:257, at], (16, 128))
            send[pl.ds(a * 256 + 10, 16, stride=16), :] = jnp.broadcast_to(got[257:258, at], (16, 128))
    got = nt(lhs[...], pt[1024:1152, :])
    value = got[0:128] + got[128:256]
    sub = lax.broadcasted_iota(I32, (8, 128), 0)
    group = lax.broadcasted_iota(I32, (8, 128), 1) >> 4
    for j in range(16):
        x = value[8 * j : 8 * j + 8]
        for m in (1, 2, 4):
            up = pltpu.roll(pltpu.roll(x, 8 - m, 0), 16 * m, 1)
            down = pltpu.roll(pltpu.roll(x, m, 0), 128 - 16 * m, 1)
            i_bit, a_bit = (sub & m) != 0, (group & m) != 0
            x = jnp.where(i_bit == a_bit, x, jnp.where(a_bit, up, down))
        send[pl.ds(j * 16 + 8, 8, stride=256), :] = x
    cell, off = got[256:257], got[257:258]
    for a in range(8):
        first = pltpu.roll(cell, (128 - 16 * a) % 128, 1) if a else cell
        second = pltpu.roll(off, (144 - 16 * a) % 128, 1) if a != 1 else off
        row = jnp.where(lane < 16, first, second)
        send[pl.ds(a * 256 + 11, 16, stride=16), :] = jnp.broadcast_to(row, (16, 128))


def factors(vert_ref, zf, zhi, zlo, vw):
    @pl.loop(0, 8)
    def _(p):
        rows = pl.ds(pl.multiple_of(p * 128, 128), 128)
        for q in range(8):
            hi, lo = split(zf[128 * q : 128 * q + 128, rows].T)
            zhi[rows, 128 * q : 128 * q + 128] = hi
            zlo[rows, 128 * q : 128 * q + 128] = lo

    for f in range(4):
        v = jnp.concatenate([vert_ref[f, pl.ds(s, 32, stride=4), :] for s in range(4)], axis=0)
        hi, lo = split(v)
        vw[128 * f : 128 * f + 128, 0:128] = hi
        vw[128 * f : 128 * f + 128, 128:256] = lo


def scatter(share, recv, tv, t8, tc, to, t11, am, lm, adj):
    for i in range(8):
        tv[pl.ds(i, 128, stride=8), :] = recv[pl.ds(i, 128, stride=16), :].T
    t8[...] = recv[pl.ds(8, 128, stride=16), :].T
    tc[...] = recv[pl.ds(9, 128, stride=16), :].T
    to[...] = recv[pl.ds(10, 128, stride=16), :].T
    t11[...] = recv[pl.ds(11, 128, stride=16), :].T
    sub = lax.broadcasted_iota(I32, (8, 128), 0)

    def block(b):
        for k in range(9):
            if k < 8:
                v = tv[pl.ds(pl.multiple_of((k * 16 + b) * 8, 8), 8), :]
                cell, off = tc[pl.ds(k * 16 + b, 1), :], to[pl.ds(k * 16 + b, 1), :]
            else:
                v = t8[pl.ds(b, 8, stride=16), :]
                cell, off = t11[pl.ds(b, 1), :], t11[pl.ds(16 + b, 1), :]
            cell, off = cell.astype(I32), off.astype(I32)
            first = (off - share + 3) >> 2
            code = (cell >> 6) * 4 + ((first + 7 - sub) >> 3)
            hi = v.astype(BF16).astype(F32)
            lo = v - hi
            at = slice(128 * k, 128 * k + 128)
            hits = [code == n for n in range(16)]
            am[0:128, at] = jnp.concatenate([jnp.where(h, hi, 0.0) for h in hits], axis=0).astype(BF16)
            am[128:256, at] = jnp.concatenate([jnp.where(h, lo, 0.0) for h in hits], axis=0).astype(BF16)
            lm[:, at] = onehot(64, cell & 63)
        got = nt(am[...], lm[...])
        return got[0:128] + got[128:256]

    @pl.loop(0, 8)
    def _(pair):
        both = jnp.concatenate([block(2 * pair), block(2 * pair + 1)], axis=1)
        hi, lo = split(both)
        at = pl.ds(pl.multiple_of(pair * 128, 128), 128)
        adj[0:128, at] = hi
        adj[128:256, at] = lo


def kernel(
    count_ref, dest_ref, cell_ref, off_ref, dep_ref, rinv_ref, w_ref, vert_ref, z_hbm, control_hbm, out_ref,
    wt, lhs, pt, send, recv, zf, zhi, zlo, vw, tv, t8, tc, to, t11, am, lm, adj, zon, back, control,
    send_sem, recv_sem, send2_sem, recv2_sem, load_sem,
):
    la, lo = lax.axis_index("lat"), lax.axis_index("lon")
    me = la * 16 + lo
    barrier = pltpu.get_barrier_semaphore()
    for o in ALL:
        pl.semaphore_signal(barrier, inc=1, device_id=peer(la, lo, o), device_id_type=MESH)
    load_z = pltpu.make_async_copy(z_hbm, zf, load_sem.at[0])
    load_z.start()
    load_control = pltpu.make_async_copy(control_hbm, control, load_sem.at[1])
    load_control.start()

    prepare(count_ref, dest_ref, cell_ref, off_ref, dep_ref, rinv_ref, w_ref, wt, lhs, pt, send)

    def rows16(p):
        return pl.ds(pl.multiple_of(p * 16, 16), MSG)

    pl.semaphore_wait(barrier, len(ALL))
    copies = []
    for o in ALL:
        to_lat, to_lon = peer(la, lo, o)
        p = to_lat * 16 + to_lon
        copy = pltpu.make_async_remote_copy(
            src_ref=send.at[rows16(p)],
            dst_ref=recv.at[rows16(me)],
            send_sem=send_sem.at[p],
            recv_sem=recv_sem.at[me],
            device_id=(to_lat, to_lon),
            device_id_type=MESH,
        )
        copy.start()
    recv[pl.ds(pl.multiple_of(me * 16, 16), 16), :] = send[pl.ds(pl.multiple_of(me * 16, 16), 16), :]

    load_z.wait()
    factors(vert_ref, zf, zhi, zlo, vw)

    def arrived(step, _):
        p = (me + step) % 128
        pltpu.make_async_remote_copy(
            src_ref=send.at[rows16(p)], dst_ref=recv.at[rows16(p)], send_sem=send_sem.at[p], recv_sem=recv_sem.at[p],
            device_id=(p // 16, p % 16), device_id_type=MESH,
        ).wait_recv()
        return 0

    lax.fori_loop(1, 128, arrived, 0)
    scatter(lo % 4, recv, tv, t8, tc, to, t11, am, lm, adj)

    for n in range(4):
        at = slice(256 * n, 256 * n + 256)
        got = nt(zhi[at, :], adj[...])
        zon[at, :] = got[:, 0:128] + got[:, 128:256] + nt(zlo[at, :], adj[0:128, :])

    def rows64(p):
        return pl.ds(pl.multiple_of(p * 64, 64), 64)

    def returned(p, q):
        return pltpu.make_async_remote_copy(
            src_ref=zon.at[rows64(p)], dst_ref=back.at[rows64(q)], send_sem=send2_sem.at[p], recv_sem=recv2_sem.at[q],
            device_id=(la, p), device_id_type=MESH,
        )

    for o in BAND:
        returned(peer(la, lo, o)[1], lo).start()
    back[rows64(lo), :] = zon[rows64(lo), :]
    load_control.wait()

    def come_back(step, _):
        p = (lo + step) % 16
        returned(p, p).wait_recv()
        return 0

    lax.fori_loop(1, 16, come_back, 0)
    group = lax.broadcasted_iota(I32, (64, 128), 1) >> 5
    for f in range(4):
        parts = [back[64 * (4 * f + s) : 64 * (4 * f + s) + 64, :] for s in range(4)]
        rows = []
        for r in range(4):
            x = parts[0] if r == 0 else pltpu.roll(parts[0], 128 - 32 * r, 1)
            for s in range(1, 4):
                y = parts[s] if s == r else pltpu.roll(parts[s], (32 * (s - r)) % 128, 1)
                x = jnp.where(group == s, y, x)
            rows.append(x)
        hi, low = split(jnp.concatenate(rows, axis=0))
        w = vw[128 * f : 128 * f + 128, :]
        got = nn(hi, w)
        got = got[:, 0:128] + got[:, 128:256] + nn(low, w[:, 0:128])
        out_ref[:, 128 * f : 128 * f + 128] = control[:, 128 * f : 128 * f + 128] + got

    def sent(step, _):
        p = (me + step) % 128
        pltpu.make_async_remote_copy(
            src_ref=send.at[rows16(p)], dst_ref=recv.at[rows16(p)], send_sem=send_sem.at[p], recv_sem=recv_sem.at[p],
            device_id=(p // 16, p % 16), device_id_type=MESH,
        ).wait_send()
        return 0

    lax.fori_loop(1, 128, sent, 0)

    def sent_back(step, _):
        p = (lo + step) % 16
        returned(p, p).wait_send()
        return 0

    lax.fori_loop(1, 16, sent_back, 0)


def per_device(
    control, vert_factor, zonal_factor, obs_dest, obs_cell, obs_offset, obs_count, departure, obs_rinv, obs_weights
):
    vmem = pl.BlockSpec(memory_space=pltpu.VMEM)
    anywhere = pl.BlockSpec(memory_space=pl.ANY)
    out = pl.pallas_call(
        kernel,
        out_shape=jax.ShapeDtypeStruct((256, 512), F32),
        in_specs=[pl.BlockSpec(memory_space=pltpu.SMEM)] + [vmem] * 7 + [anywhere] * 2,
        out_specs=vmem,
        scratch_shapes=[
            pltpu.VMEM((N_OBS, 128), F32),
            pltpu.VMEM((272, N_OBS), BF16),
            pltpu.VMEM((SLOTS, N_OBS), BF16),
            pltpu.VMEM((2048, 128), F32),
            pltpu.VMEM((2048, 128), F32),
            pltpu.VMEM((1024, 1024), F32),
            pltpu.VMEM((1024, 1024), BF16),
            pltpu.VMEM((1024, 1024), BF16),
            pltpu.VMEM((512, 256), BF16),
            pltpu.VMEM((1024, 128), F32),
            pltpu.VMEM((128, 128), F32),
            pltpu.VMEM((128, 128), F32),
            pltpu.VMEM((128, 128), F32),
            pltpu.VMEM((128, 128), F32),
            pltpu.VMEM((256, SLOTS), BF16),
            pltpu.VMEM((64, SLOTS), BF16),
            pltpu.VMEM((256, 1024), BF16),
            pltpu.VMEM((1024, 128), F32),
            pltpu.VMEM((1024, 128), F32),
            pltpu.VMEM((256, 512), F32),
            pltpu.SemaphoreType.DMA((128,)),
            pltpu.SemaphoreType.DMA((128,)),
            pltpu.SemaphoreType.DMA((16,)),
            pltpu.SemaphoreType.DMA((16,)),
            pltpu.SemaphoreType.DMA((2,)),
        ],
        compiler_params=pltpu.CompilerParams(
            collective_id=0, has_side_effects=True, vmem_limit_bytes=48 * 2**20
        ),
        name="gradient",
    )(
        obs_count,
        obs_dest.reshape(1, N_OBS),
        obs_cell.reshape(1, N_OBS),
        obs_offset.reshape(1, N_OBS),
        departure.reshape(1, N_OBS),
        obs_rinv.reshape(1, N_OBS),
        obs_weights,
        vert_factor,
        zonal_factor,
        control.reshape(256, 512),
    )
    return out.reshape(4, 64, 512)


def solution(mesh):
    return jax.shard_map(
        per_device,
        mesh=mesh,
        in_specs=(
            P("lat", "lon", None),
            P(),
            P(),
            P(("lat", "lon"), None),
            P(("lat", "lon")),
            P(("lat", "lon")),
            P(("lat", "lon")),
            P(("lat", "lon")),
            P(("lat", "lon")),
            P(("lat", "lon"), None),
        ),
        out_specs=P("lat", "lon", None),
        check_vma=False,
    )
```

time: 147 us -> 53.9 us (0.37); the launches traced: 144 us -> 53.5 us
  waiting for transfers between devices: 50.8 us -> 0 us
  Pallas kernels: 0 us -> 43.4 us
  blocking collectives: 25.1 us -> 0 us
  starting transfers between devices: 21.7 us -> 0 us
  matrix products: 17.6 us -> 0 us
  local copies, waits for them, and re-layouts: 19.7 us -> 9.41 us
  other arithmetic: 8.46 us -> 0 us
    all_to_all x2 -> x0, waiting for transfers between devices: 50.8 us -> none  [the longest x1 50.8 us: per_device(): lax.all_to_all(payload.reshape(devices, capacity, width), ('lat', 'lon'),...]
    pallas_call x0 -> x1, Pallas kernels: none -> 43.4 us  [per_device(): pl.pallas_call(kernel, out_shape=jax.ShapeDtypeStruct((256, 512), F32), i...]
    all_to_all x2 -> x0, blocking collectives: 25.1 us -> none  [the longest x1 13.2 us: per_device(): lax.all_to_all(product, 'lon', split_axis=2, concat_axis=1, tiled=True)]
    all_to_all x2 -> x0, starting transfers between devices: 21.7 us -> none  [the longest x1 11.5 us: per_device(): lax.all_to_all(labels.reshape(devices, capacity, label_width), ('lat', 'l...]
    dot_general x5 -> x0, matrix products: 17.6 us -> none  [the longest x1 6.12 us: place_levels(): jnp.einsum('rfk,rkl->rfl', blocks, shift_mat, precision=lax.Precision.HIG...]
    dot_general x3 -> x0, local copies, waits for them, and re-layouts: 6.29 us -> none  [the longest x1 3.45 us: per_device(): payload = jnp.dot(slot_mat, profile, precision=lax.Precision.HIGHEST)]
    all_to_all x3 -> x0, other arithmetic: 4.58 us -> none  [the longest x1 1.89 us: per_device(): lax.all_to_all(product, 'lon', split_axis=2, concat_axis=1, tiled=True)]
    all_to_all x7 -> x0, local copies, waits for them, and re-layouts: 3.15 us -> none  [the longest x4 1.5 us: per_device(): lax.all_to_all(vertical, 'lon', split_axis=1, concat_axis=2, tiled=True)]
  transfers between devices with their start and end apart: 2 -> 0, of which waited for: 1 -> 0; matrix products, arithmetic and copies ran while one was open for 11% -> 0% of each run, Pallas kernels for 0% -> 0%
where the time goes in v1:
time: 53.9 us; the launch traced here: 53.5 us
  Pallas kernels  43.4 us (81%)
  local copies, waits for them, and re-layouts  9.41 us (17%)
  between operations  0.67 us (1%)
    pallas_call x1, Pallas kernels, per_device(): pl.pallas_call(kernel, out_shape=jax.ShapeDtypeStruct((256, 512), F32), i...  43.4 us
    unnamed x11, local copies, waits for them, and re-layouts  6.65 us

profile of v1, /device:TPU:1, one launch (start us, length us, event | category | flops | bytes accessed | tf_op | source)
XLA Modules:
  0.0 53.5 jit_solution(6486919287793595408)
XLA Ops:
  0.7 0.7 %reshape.22.cell_ref = s32[1,768]{1,0:T(1,128)S(1)} reshape(s32[768]{0:T(1024)} %param.14) | data formatting | bytes 6144 | tf_op jit(solution)/shard_map/reshape | solution.py:342
  1.3 0.7 %reshape.23.off_ref = s32[1,768]{1,0:T(1,128)S(1)} reshape(s32[768]{0:T(1024)} %param.15) | data formatting | bytes 6144 | tf_op jit(solution)/shard_map/reshape | solution.py:343
  2.0 0.7 %reshape.24.dep_ref = f32[1,768]{1,0:T(1,128)S(1)} reshape(f32[768]{0:T(1024)} %param.17) | data formatting | bytes 6144 | tf_op jit(solution)/shard_map/reshape | solution.py:344
  2.7 0.7 %reshape.25.rinv_ref = f32[1,768]{1,0:T(1,128)S(1)} reshape(f32[768]{0:T(1024)} %param.18) | data formatting | bytes 6144 | tf_op jit(solution)/shard_map/reshape | solution.py:345
  3.4 0.0 copy-start
  3.4 2.2 %copy-done = f32[1024,1024]{1,0:T(8,128)S(1)} copy-done((f32[1024,1024]{1,0:T(8,128)S(1)}, f32[1024,1024]{1,0:T(8,128)}, u32[]{:S(2)}) %copy-start) | copy-done | bytes 4194328
  5.6 0.0 copy-start.1
  5.6 1.0 %copy-done.1 = f32[4,64,512]{2,1,0:T(8,128)S(1)} copy-done((f32[4,64,512]{2,1,0:T(8,128)S(1)}, f32[4,64,512]{2,1,0:T(8,128)}, u32[]{:S(2)}) %copy-start.1) | copy-done | bytes 524312
  6.6 0.0 copy-start.2
  6.6 1.0 %copy-done.2 = f32[768,128]{1,0:T(8,128)S(1)} copy-done((f32[768,128]{1,0:T(8,128)S(1)}, f32[768,128]{1,0:T(8,128)}, u32[]{:S(2)}) %copy-start.2) | copy-done | bytes 393240
  7.6 0.0 copy-start.3
  7.6 0.9 %copy-done.3 = f32[4,128,128]{2,1,0:T(8,128)S(1)} copy-done((f32[4,128,128]{2,1,0:T(8,128)S(1)}, f32[4,128,128]{2,1,0:T(8,128)}, u32[]{:S(2)}) %copy-start.3) | copy-done | bytes 262168
  8.6 0.0 copy-start.4
  8.6 0.7 %copy-done.4 = s32[768,1]{0,1:T(1,128)S(1)} copy-done((s32[768,1]{0,1:T(1,128)S(1)}, s32[768,1]{0,1:T(1,128)}, u32[]{:S(2)}) %copy-start.4) | copy-done | bytes 3096
  9.3 43.4 %gradient.1 = f32[256,512]{1,0:T(8,128)S(1)} custom-call(s32[1]{0:T(128)S(6)} %copy.12.count_ref, s32[1,768]{1,0:T(1,128)S(1)} %bitcast.5, s32[1,768]{1,0:T(1,128)S(1)} %reshape.22.cell_ref, s32[1,768]{1,0:T(1,128)S(1)} %reshape.23.off_ref, f32[1,768]{1,0:T(1,128)S(1)} %reshape.24.dep_ref, f32[1,768]{1,0:T(1,128)S(1)} %reshape.25.rinv_ref, ...), custom_call_target="tpu_custom_call" | custom-call | tf_op jit(solution)/shard_map/gradient/pallas_call | solution.py:303
  52.7 0.8 %copy.13 = f32[4,64,512]{2,1,0:T(8,128)} copy(f32[4,64,512]{2,1,0:T(8,128)S(1)} %bitcast.3) | data formatting | bytes 1048576
Async XLA Ops:
  3.4 2.2 %copy-start = (f32[1024,1024]{1,0:T(8,128)S(1)}, f32[1024,1024]{1,0:T(8,128)}, u32[]{:S(2)}) copy-start(f32[1024,1024]{1,0:T(8,128)} %z_hbm.1) | copy-start | bytes 12582916
  5.6 1.0 %copy-start.1 = (f32[4,64,512]{2,1,0:T(8,128)S(1)}, f32[4,64,512]{2,1,0:T(8,128)}, u32[]{:S(2)}) copy-start(f32[4,64,512]{2,1,0:T(8,128)} %param.10) | copy-start | bytes 1572868
  6.6 1.0 %copy-start.2 = (f32[768,128]{1,0:T(8,128)S(1)}, f32[768,128]{1,0:T(8,128)}, u32[]{:S(2)}) copy-start(f32[768,128]{1,0:T(8,128)} %w_ref.1) | copy-start | bytes 1179652
  7.6 0.9 %copy-start.3 = (f32[4,128,128]{2,1,0:T(8,128)S(1)}, f32[4,128,128]{2,1,0:T(8,128)}, u32[]{:S(2)}) copy-start(f32[4,128,128]{2,1,0:T(8,128)} %vert_ref.1) | copy-start | bytes 786436
  8.6 0.7 %copy-start.4 = (s32[768,1]{0,1:T(1,128)S(1)}, s32[768,1]{0,1:T(1,128)}, u32[]{:S(2)}) copy-start(s32[768,1]{0,1:T(1,128)} %param.13) | copy-start | bytes 9220

commit v2 on v1

v2 whole, which is shorter than its diff:
```python
import functools

import jax
import jax.numpy as jnp
from jax import lax
from jax.experimental import pallas as pl
from jax.experimental.pallas import tpu as pltpu
from jax.sharding import PartitionSpec as P

MESH = pl.DeviceIdType.MESH
F32, BF16, I32 = jnp.float32, jnp.bfloat16, jnp.int32
N_OBS = 768
CHUNKS = N_OBS // 128
SLOTS = 1152
MSG = 12
NT = (((1,), (1,)), ((), ()))


def ring(o):
    return min(o, 4 - o)


def offsets():
    found = [(z, c, x, y) for z in range(4) for c in range(2) for x in range(4) for y in range(4)][1:]
    return sorted(found, key=lambda o: ((o[0] + o[2] + o[3]) % 4, -(ring(o[0]) + ring(o[2]) + ring(o[3]))))


ALL = offsets()


def peer(la, lo, o):
    z, c, x, y = o
    lat = (la // 2 + z) % 4 * 2 + (la % 2 + c) % 2
    lon = (lo // 4 + x) % 4 * 4 + (lo % 4 + y) % 4
    return lat, lon


def split(x):
    hi = x.astype(BF16)
    return hi, (x - hi.astype(F32)).astype(BF16)


def nt(a, b):
    return lax.dot_general(a, b, NT, preferred_element_type=F32)


def nn(a, b):
    return jnp.dot(a, b, preferred_element_type=F32)


def onehot(rows, index):
    ids = lax.broadcasted_iota(I32, (rows, 128), 0)
    return jnp.where(ids == index, 1.0, 0.0).astype(BF16)


def swap_groups(x):
    sub = lax.broadcasted_iota(I32, (8, 128), 0)
    group = lax.broadcasted_iota(I32, (8, 128), 1) >> 4
    for m in (1, 2, 4):
        up = pltpu.roll(pltpu.roll(x, 8 - m, 0), 16 * m, 1)
        down = pltpu.roll(pltpu.roll(x, m, 0), 128 - 16 * m, 1)
        i_bit, a_bit = (sub & m) != 0, (group & m) != 0
        x = jnp.where(i_bit == a_bit, x, jnp.where(a_bit, up, down))
    return x


def prepare(count_ref, dest_ref, cell_ref, off_ref, dep_ref, rinv_ref, w_ref, wt, lhs, pt, labels, send):
    lane = lax.broadcasted_iota(I32, (1, 128), 1)
    rows = lax.broadcasted_iota(I32, (128, 128), 0)
    cols = lax.broadcasted_iota(I32, (128, 128), 1)
    before = jnp.concatenate(
        [jnp.where(rows < cols, 1.0, 0.0), jnp.ones((128, 128), F32)], axis=1
    ).astype(BF16)
    earlier = jnp.zeros((128, 128), F32)
    for c in range(CHUNKS):
        at = slice(128 * c, 128 * c + 128)
        dest = dest_ref[:, at]
        cell, off, dep, rinv = (r[at].reshape(1, 128) for r in (cell_ref, off_ref, dep_ref, rinv_ref))
        scaled = jnp.where(lane + 128 * c < count_ref[0], rinv * dep, 0.0)
        wt[at, :] = w_ref[at, :].T * scaled
        mine = rows == dest
        counts = nn(jnp.where(mine, 1.0, 0.0).astype(BF16), before)
        rank = jnp.sum(jnp.where(mine, counts[:, :128] + earlier, 0.0), axis=0, keepdims=True)
        earlier = earlier + counts[:, 128:]
        pt[:, at] = onehot(SLOTS, rank.astype(I32) * 128 + dest)
        residue, turn = off & 3, off >> 2
        residue, turn = jnp.broadcast_to(residue, (8, 128)), jnp.broadcast_to(turn, (8, 128))
        shares = []
        for f in range(4):
            part = [wt[pl.ds(128 * c + 32 * f + k, 8, stride=4), :] for k in range(4)]
            for s in range(4):
                x = part[s]
                for e in range(1, 4):
                    x = jnp.where(residue == e, part[(s - e) % 4], x)
                by = turn + jnp.where(residue > s, 1, 0)
                for m in (1, 2, 4):
                    x = jnp.where((by & m) != 0, pltpu.roll(x, m, 0), x)
                shares.append(x)
        hi, lo = split(jnp.concatenate(shares, axis=0))
        lhs[0:128, at] = hi
        lhs[128:256, at] = lo
        ids = lax.broadcasted_iota(I32, (16, 128), 0)
        lhs[256:272, at] = jnp.where(ids == 0, cell, jnp.where(ids == 1, off, 0)).astype(F32).astype(BF16)

    for k in range(0, 9, 2):
        got = nt(lhs[...], pt[128 * k : min(128 * k + 256, SLOTS), :])
        value = got[0:128] + got[128:256]
        for half in range(2 if k < 8 else 1):
            at = slice(128 * half, 128 * half + 128)
            for j in range(16):
                send[pl.ds(j * 16 + k + half, 8, stride=256), :] = swap_groups(value[8 * j : 8 * j + 8, at])
            labels[pl.ds(k + half, 1), :] = got[256:257, at]
            labels[pl.ds(16 + k + half, 1), :] = got[257:258, at]
    cell, off = swap_groups(labels[0:8, :]), swap_groups(labels[16:24, :])
    cell8, off8 = labels[8:9, :], labels[24:25, :]
    for a in range(8):
        first = pltpu.roll(cell8, (128 - 16 * a) % 128, 1) if a else cell8
        second = pltpu.roll(off8, (144 - 16 * a) % 128, 1) if a != 1 else off8
        last = jnp.where(lane < 16, first, second)
        for at, row in ((9, cell[a : a + 1]), (10, off[a : a + 1]), (11, last)):
            send[pl.ds(a * 256 + at, 16, stride=16), :] = jnp.broadcast_to(row, (16, 128))


def factors(vert_ref, zf, zhi, zlo, vw):
    @pl.loop(0, 8)
    def _(p):
        rows = pl.ds(pl.multiple_of(p * 128, 128), 128)
        for q in range(8):
            hi, lo = split(zf[128 * q : 128 * q + 128, rows].T)
            zhi[rows, 128 * q : 128 * q + 128] = hi
            zlo[rows, 128 * q : 128 * q + 128] = lo

    for f in range(4):
        v = jnp.concatenate([vert_ref[f, pl.ds(s, 32, stride=4), :] for s in range(4)], axis=0)
        hi, lo = split(v)
        vw[128 * f : 128 * f + 128, 0:128] = hi
        vw[128 * f : 128 * f + 128, 128:256] = lo


def scatter(share, base, last, recv, tv, tm, am, lm, acc):
    tiles = 3 if last else 2
    lane = lax.broadcasted_iota(I32, (16, 128), 1)
    for t in range(2):
        value = [recv[pl.ds(base + 4 * t + k, 32, stride=16), :] for k in range(4)]
        tv[128 * t : 128 * t + 128, :] = jnp.concatenate(value, axis=0).T
    for n in range(2):
        by_source = recv[pl.ds(base + 9 + n, 32, stride=16), :]
        labels = jnp.concatenate([by_source, jnp.zeros((96, 128), F32)], axis=0).T
        for t in range(2):
            x = labels[64 * t : 64 * t + 16]
            for k in range(1, 4):
                r = 64 * t + 16 * k
                x = jnp.where(lane < 32 * k, x, pltpu.roll(labels[r : r + 16], 32 * k, 1))
            tm[32 * t + 16 * n : 32 * t + 16 * n + 16, :] = x
    if last:
        tv[256:384, :] = recv[pl.ds(8, 128, stride=16), :].T
        tm[64:192, :] = recv[pl.ds(11, 128, stride=16), :].T
    sub = lax.broadcasted_iota(I32, (8, 128), 0)

    @pl.loop(0, 8)
    def _(pair):
        for half in range(2):
            b = 2 * pair + half
            for t in range(tiles):
                v = tv[pl.ds(128 * t + b, 8, stride=16), :]
                cell, off = tm[pl.ds(32 * t + b, 1), :], tm[pl.ds(32 * t + 16 + b, 1), :]
                cell, off = cell.astype(I32), off.astype(I32)
                first = (off - share + 3) >> 2
                code = (cell >> 6) * 4 + ((first + 7 - sub) >> 3)
                hi = v.astype(BF16).astype(F32)
                lo = v - hi
                k = tiles * half + t
                at = slice(128 * k, 128 * k + 128)
                hits = [code == n for n in range(16)]
                am[0:128, at] = jnp.concatenate([jnp.where(h, hi, 0.0) for h in hits], axis=0).astype(BF16)
                am[128:256, at] = jnp.concatenate([jnp.where(h, lo, 0.0) for h in hits], axis=0).astype(BF16)
                lm[:, at] = onehot(128, (cell & 63) + 64 * half)
        at = slice(0, 256 * tiles)
        acc[pair] += nt(am[:, at], lm[:, at])


def kernel(
    count_ref, dest_hbm, cell_hbm, off_hbm, dep_hbm, rinv_hbm, w_hbm, vert_hbm, z_hbm, control_hbm, out_ref,
    dest_ref, cell_ref, off_ref, dep_ref, rinv_ref, w_ref, vert_ref, zf, control,
    wt, lhs, pt, labels, send, recv, zhi, zlo, vw, tv, tm, am, lm, acc, adj, zon, back,
    send_sem, recv_sem, send2_sem, recv2_sem, load_sem,
):
    la, lo = lax.axis_index("lat"), lax.axis_index("lon")
    z, x, y = la // 2, lo // 4, lo % 4
    barrier = pltpu.get_barrier_semaphore()
    for o in ALL:
        pl.semaphore_signal(barrier, inc=1, device_id=peer(la, lo, o), device_id_type=MESH)
    loads = [
        pltpu.make_async_copy(src, dst, load_sem.at[n])
        for n, (src, dst) in enumerate(
            (
                (w_hbm, w_ref), (dest_hbm, dest_ref), (cell_hbm, cell_ref), (off_hbm, off_ref), (dep_hbm, dep_ref),
                (rinv_hbm, rinv_ref), (vert_hbm, vert_ref), (z_hbm, zf), (control_hbm, control),
            )
        )
    ]
    for load in loads:
        load.start()
    for load in loads[:6]:
        load.wait()

    prepare(count_ref, dest_ref, cell_ref, off_ref, dep_ref, rinv_ref, w_ref, wt, lhs, pt, labels, send)

    def rows16(p):
        return pl.ds(pl.multiple_of(p * 16, 16), MSG)

    def place(x, y, z, c):
        return (x + y + z) % 4 * 32 + (x * 4 + y) * 2 + c

    me = place(x, y, z, la % 2)
    pl.semaphore_wait(barrier, len(ALL))

    def message(p, q, device):
        return pltpu.make_async_remote_copy(
            src_ref=send.at[rows16(p)], dst_ref=recv.at[rows16(q)], send_sem=send_sem.at[p], recv_sem=recv_sem.at[q],
            device_id=device, device_id_type=MESH,
        )

    for o in ALL:
        to_lat, to_lon = peer(la, lo, o)
        message(to_lat * 16 + to_lon, me, (to_lat, to_lon)).start()
    mine = pl.ds(pl.multiple_of((la * 16 + lo) * 16, 16), 16)
    recv[pl.ds(pl.multiple_of(me * 16, 16), 16), :] = send[mine, :]

    for load in loads[6:8]:
        load.wait()
    factors(vert_ref, zf, zhi, zlo, vw)
    acc[...] = jnp.zeros_like(acc)

    other = ((la + 1) % 8, lo)
    for k in range(4):
        key = (x + y + z + 4 - k) % 4

        def arrived(step, _):
            q = key * 32 + (me + step) % 32
            message(q, q, other).wait_recv()
            return 0

        lax.fori_loop(0 if k else 1, 32, arrived, 0)
        scatter(lo % 4, pl.multiple_of(key * 512, 512), k == 3, recv, tv, tm, am, lm, acc)
    for pair in range(8):
        hi, low = split(acc[pair, 0:128, :] + acc[pair, 128:256, :])
        adj[0:128, 128 * pair : 128 * pair + 128] = hi
        adj[128:256, 128 * pair : 128 * pair + 128] = low

    def rows64(p):
        return pl.ds(pl.multiple_of(p * 64, 64), 64)

    def returned(p, q):
        return pltpu.make_async_remote_copy(
            src_ref=zon.at[rows64(p)], dst_ref=back.at[rows64(q)], send_sem=send2_sem.at[p], recv_sem=recv2_sem.at[q],
            device_id=(la, p), device_id_type=MESH,
        )

    for ox in (2, 1, 3, 0):
        to_x = (x + ox) % 4
        at = pl.ds(pl.multiple_of(to_x * 256, 256), 256)
        got = nt(zhi[at, :], adj[...])
        zon[at, :] = got[:, 0:128] + got[:, 128:256] + nt(zlo[at, :], adj[0:128, :])
        for oy in (2, 1, 3, 0):
            if (ox, oy) != (0, 0):
                returned(to_x * 4 + (y + oy) % 4, lo).start()
    back[rows64(lo), :] = zon[rows64(lo), :]
    loads[8].wait()

    group = lax.broadcasted_iota(I32, (64, 128), 1) >> 5
    for ox in (2, 3, 1, 0):
        f = (x + ox) % 4
        for oy in (2, 3, 1, 0):
            if (ox, oy) != (0, 0):
                p = f * 4 + (y + oy) % 4
                returned(p, p).wait_recv()
        parts = [back[pl.ds(pl.multiple_of(f * 256 + 64 * s, 64), 64), :] for s in range(4)]
        rows = []
        for r in range(4):
            got = parts[0] if r == 0 else pltpu.roll(parts[0], 128 - 32 * r, 1)
            for s in range(1, 4):
                turned = parts[s] if s == r else pltpu.roll(parts[s], (32 * (s - r)) % 128, 1)
                got = jnp.where(group == s, turned, got)
            rows.append(got)
        hi, low = split(jnp.concatenate(rows, axis=0))
        at = pl.ds(pl.multiple_of(f * 128, 128), 128)
        w = vw[at, :]
        got = nn(hi, w)
        got = got[:, 0:128] + got[:, 128:256] + nn(low, w[:, 0:128])
        out_ref[:, at] = control[:, at] + got

    def sent(step, _):
        p = (la * 16 + lo + step) % 128
        message(p, p, other).wait_send()
        return 0

    lax.fori_loop(1, 128, sent, 0)

    def sent_back(step, _):
        p = (lo + step) % 16
        returned(p, p).wait_send()
        return 0

    lax.fori_loop(1, 16, sent_back, 0)


def per_device(
    control, vert_factor, zonal_factor, obs_dest, obs_cell, obs_offset, obs_count, departure, obs_rinv, obs_weights
):
    anywhere = pl.BlockSpec(memory_space=pl.ANY)
    out = pl.pallas_call(
        kernel,
        out_shape=jax.ShapeDtypeStruct((256, 512), F32),
        in_specs=[pl.BlockSpec(memory_space=pltpu.SMEM)] + [anywhere] * 9,
        out_specs=pl.BlockSpec(memory_space=pltpu.VMEM),
        scratch_shapes=[
            pltpu.VMEM((1, N_OBS), I32),
            pltpu.VMEM((N_OBS,), I32),
            pltpu.VMEM((N_OBS,), I32),
            pltpu.VMEM((N_OBS,), F32),
            pltpu.VMEM((N_OBS,), F32),
            pltpu.VMEM((N_OBS, 128), F32),
            pltpu.VMEM((4, 128, 128), F32),
            pltpu.VMEM((1024, 1024), F32),
            pltpu.VMEM((256, 512), F32),
            pltpu.VMEM((N_OBS, 128), F32),
            pltpu.VMEM((272, N_OBS), BF16),
            pltpu.VMEM((SLOTS, N_OBS), BF16),
            pltpu.VMEM((32, 128), F32),
            pltpu.VMEM((2048, 128), F32),
            pltpu.VMEM((2048, 128), F32),
            pltpu.VMEM((1024, 1024), BF16),
            pltpu.VMEM((1024, 1024), BF16),
            pltpu.VMEM((512, 256), BF16),
            pltpu.VMEM((384, 128), F32),
            pltpu.VMEM((192, 128), F32),
            pltpu.VMEM((256, 768), BF16),
            pltpu.VMEM((128, 768), BF16),
            pltpu.VMEM((8, 256, 128), F32),
            pltpu.VMEM((256, 1024), BF16),
            pltpu.VMEM((1024, 128), F32),
            pltpu.VMEM((1024, 128), F32),
            pltpu.SemaphoreType.DMA((128,)),
            pltpu.SemaphoreType.DMA((128,)),
            pltpu.SemaphoreType.DMA((16,)),
            pltpu.SemaphoreType.DMA((16,)),
            pltpu.SemaphoreType.DMA((9,)),
        ],
        compiler_params=pltpu.CompilerParams(
            collective_id=0, has_side_effects=True, vmem_limit_bytes=60 * 2**20
        ),
        name="gradient",
    )(
        obs_count,
        obs_dest.reshape(1, N_OBS),
        obs_cell,
        obs_offset,
        departure,
        obs_rinv,
        obs_weights,
        vert_factor,
        zonal_factor,
        control.reshape(256, 512),
    )
    return out.reshape(4, 64, 512)


def solution(mesh):
    return jax.shard_map(
        per_device,
        mesh=mesh,
        in_specs=(
            P("lat", "lon", None),
            P(),
            P(),
            P(("lat", "lon"), None),
            P(("lat", "lon")),
            P(("lat", "lon")),
            P(("lat", "lon")),
            P(("lat", "lon")),
            P(("lat", "lon")),
            P(("lat", "lon"), None),
        ),
        out_specs=P("lat", "lon", None),
        check_vma=False,
    )
```

time: 53.9 us -> 47.5 us (0.88)
  local copies, waits for them, and re-layouts: 9.41 us -> 1.87 us
  Pallas kernels: 43.4 us -> 44.8 us
    unnamed x11 -> x1, local copies, waits for them, and re-layouts: 6.65 us -> 1.87 us
    reshape x4 -> x0, local copies, waits for them, and re-layouts: 2.76 us -> none  [the longest x1 0.69 us: per_device(): obs_cell.reshape(1, N_OBS)]
    pallas_call x1, Pallas kernels: 43.4 us -> 44.8 us  [per_device(): pl.pallas_call(kernel, out_shape=jax.ShapeDtypeStruct((256, 512), F32), i...]
where the time goes in v2:
time: 47.5 us; the launch traced here: 47.4 us
  Pallas kernels  44.8 us (94%)
  local copies, waits for them, and re-layouts  1.87 us (4%)
  between operations  0.66 us (1%)
    pallas_call x1, Pallas kernels, per_device(): pl.pallas_call(kernel, out_shape=jax.ShapeDtypeStruct((256, 512), F32), i...  44.8 us
    unnamed x1, local copies, waits for them, and re-layouts  1.87 us

profile of v2, /device:TPU:1, one launch (start us, length us, event | category | flops | bytes accessed | tf_op | source)
XLA Modules:
  0.0 47.4 jit_solution(10373386439032911282)
XLA Ops:
  0.7 44.8 %gradient.1 = f32[256,512]{1,0:T(8,128)} custom-call(s32[1]{0:T(128)S(6)} %copy.12.count_ref, s32[1,768]{1,0:T(1,128)} %bitcast.5, s32[768]{0:T(1024)} %cell_hbm.1, s32[768]{0:T(1024)} %off_hbm.1, f32[768]{0:T(1024)} %dep_hbm.1, f32[768]{0:T(1024)} %rinv_hbm.1, f32[768,128]{1,0:T(8,128)} %w_hbm.1, f32[4,128,128]{2,1,0:T(8,128)} %vert_hbm.1, ...), custom_call_target="tpu_custom_call" | custom-call | tf_op jit(solution)/shard_map/gradient/pallas_call | solution.py:312
  45.5 1.9 %copy.13 = f32[4,64,512]{2,1,0:T(8,128)} copy(f32[4,64,512]{2,1,0:T(8,128)} %bitcast.3) | data formatting | bytes 1048576

commit v3 on v2

--- a/solution.py
+++ b/solution.py
@@ -13,6 +13,7 @@
 CHUNKS = N_OBS // 128
 SLOTS = 1152
 MSG = 12
+UNROLL = 8
 NT = (((1,), (1,)), ((), ()))
 
 
@@ -137,7 +138,7 @@
         vw[128 * f : 128 * f + 128, 128:256] = lo
 
 
-def scatter(share, base, last, recv, tv, tm, am, lm, acc):
+def scatter(share, base, last, recv, tv, tm, acc):
     tiles = 3 if last else 2
     lane = lax.broadcasted_iota(I32, (16, 128), 1)
     for t in range(2):
@@ -156,34 +157,45 @@
         tv[256:384, :] = recv[pl.ds(8, 128, stride=16), :].T
         tm[64:192, :] = recv[pl.ds(11, 128, stride=16), :].T
     sub = lax.broadcasted_iota(I32, (8, 128), 0)
-
-    @pl.loop(0, 8)
-    def _(pair):
+    place = lax.broadcasted_iota(I32, (16, 128), 0).astype(F32)
+    zero = jnp.zeros((16, 128), BF16)
+    one = jnp.ones((16, 128), BF16)
+
+    def twice(x):
+        return jnp.concatenate([x, x], axis=0)
+
+    def tile(b, t):
+        v = tv[pl.ds(128 * t + b, 8, stride=16), :]
+        cell, off = tm[pl.ds(32 * t + b, 1), :], tm[pl.ds(32 * t + 16 + b, 1), :]
+        cell, off = cell.astype(I32), off.astype(I32)
+        first = (off - share + 3) >> 2
+        code = ((cell >> 6) * 4 + ((first + 7 - sub) >> 3)).astype(F32)
+        code = jnp.concatenate([code, code - 1.0], axis=0).astype(BF16)
+        hi, lo = split(twice(v))
+        hits = [code == jnp.asarray(2 * n, BF16) for n in range(8)]
+        levels = jnp.concatenate([jnp.where(h, x, zero) for x in (hi, lo) for h in hits], axis=0)
+        lon = (cell & 63).astype(F32)
+        columns = [jnp.where((lon - place - 16.0 * n).astype(BF16) == zero, one, zero) for n in range(4)]
+        return levels, jnp.concatenate(columns, axis=0)
+
+    def one_pair(pair, _):
+        parts = []
         for half in range(2):
-            b = 2 * pair + half
-            for t in range(tiles):
-                v = tv[pl.ds(128 * t + b, 8, stride=16), :]
-                cell, off = tm[pl.ds(32 * t + b, 1), :], tm[pl.ds(32 * t + 16 + b, 1), :]
-                cell, off = cell.astype(I32), off.astype(I32)
-                first = (off - share + 3) >> 2
-                code = (cell >> 6) * 4 + ((first + 7 - sub) >> 3)
-                hi = v.astype(BF16).astype(F32)
-                lo = v - hi
-                k = tiles * half + t
-                at = slice(128 * k, 128 * k + 128)
-                hits = [code == n for n in range(16)]
-                am[0:128, at] = jnp.concatenate([jnp.where(h, hi, 0.0) for h in hits], axis=0).astype(BF16)
-                am[128:256, at] = jnp.concatenate([jnp.where(h, lo, 0.0) for h in hits], axis=0).astype(BF16)
-                lm[:, at] = onehot(128, (cell & 63) + 64 * half)
-        at = slice(0, 256 * tiles)
-        acc[pair] += nt(am[:, at], lm[:, at])
+            made = [tile(2 * pair + half, t) for t in range(tiles)]
+            levels = jnp.concatenate([m[0] for m in made], axis=1)
+            columns = jnp.concatenate([m[1] for m in made], axis=1)
+            parts.append(nt(levels, columns))
+        acc[pair] += jnp.concatenate(parts, axis=1)
+        return 0
+
+    lax.fori_loop(0, 8, one_pair, 0, unroll=UNROLL)
 
 
 def kernel(
-    count_ref, dest_hbm, cell_hbm, off_hbm, dep_hbm, rinv_hbm, w_hbm, vert_hbm, z_hbm, control_hbm, out_ref,
-    dest_ref, cell_ref, off_ref, dep_ref, rinv_ref, w_ref, vert_ref, zf, control,
-    wt, lhs, pt, labels, send, recv, zhi, zlo, vw, tv, tm, am, lm, acc, adj, zon, back,
-    send_sem, recv_sem, send2_sem, recv2_sem, load_sem,
+    count_ref, dest_hbm, cell_hbm, off_hbm, dep_hbm, rinv_hbm, w_hbm, vert_hbm, z_hbm, out_ref,
+    dest_ref, cell_ref, off_ref, dep_ref, rinv_ref, w_ref, vert_ref, zf,
+    wt, lhs, pt, labels, send, recv, zhi, zlo, vw, tv, tm, acc, adj, zon, back,
+    send_sem, recv_sem, load_sem,
 ):
     la, lo = lax.axis_index("lat"), lax.axis_index("lon")
     z, x, y = la // 2, lo // 4, lo % 4
@@ -195,7 +207,7 @@
         for n, (src, dst) in enumerate(
             (
                 (w_hbm, w_ref), (dest_hbm, dest_ref), (cell_hbm, cell_ref), (off_hbm, off_ref), (dep_hbm, dep_ref),
-                (rinv_hbm, rinv_ref), (vert_hbm, vert_ref), (z_hbm, zf), (control_hbm, control),
+                (rinv_hbm, rinv_ref), (vert_hbm, vert_ref), (z_hbm, zf),
             )
         )
     ]
@@ -215,15 +227,18 @@
     me = place(x, y, z, la % 2)
     pl.semaphore_wait(barrier, len(ALL))
 
-    def message(p, q, device):
+    my_key = (x + y + z) % 4
+    other = ((la + 1) % 8, lo)
+
+    def message(src, dst, key, device):
         return pltpu.make_async_remote_copy(
-            src_ref=send.at[rows16(p)], dst_ref=recv.at[rows16(q)], send_sem=send_sem.at[p], recv_sem=recv_sem.at[q],
+            src_ref=send.at[src], dst_ref=recv.at[dst], send_sem=send_sem.at[0], recv_sem=recv_sem.at[key],
             device_id=device, device_id_type=MESH,
         )
 
     for o in ALL:
         to_lat, to_lon = peer(la, lo, o)
-        message(to_lat * 16 + to_lon, me, (to_lat, to_lon)).start()
+        message(rows16(to_lat * 16 + to_lon), rows16(me), my_key, (to_lat, to_lon)).start()
     mine = pl.ds(pl.multiple_of((la * 16 + lo) * 16, 16), 16)
     recv[pl.ds(pl.multiple_of(me * 16, 16), 16), :] = send[mine, :]
 
@@ -232,17 +247,11 @@
     factors(vert_ref, zf, zhi, zlo, vw)
     acc[...] = jnp.zeros_like(acc)
 
-    other = ((la + 1) % 8, lo)
     for k in range(4):
-        key = (x + y + z + 4 - k) % 4
-
-        def arrived(step, _):
-            q = key * 32 + (me + step) % 32
-            message(q, q, other).wait_recv()
-            return 0
-
-        lax.fori_loop(0 if k else 1, 32, arrived, 0)
-        scatter(lo % 4, pl.multiple_of(key * 512, 512), k == 3, recv, tv, tm, am, lm, acc)
+        key = (my_key + 4 - k) % 4
+        together = pl.ds(0, MSG * (32 if k else 31))
+        message(together, together, key, other).wait_recv()
+        scatter(lo % 4, pl.multiple_of(key * 512, 512), k == 3, recv, tv, tm, acc)
     for pair in range(8):
         hi, low = split(acc[pair, 0:128, :] + acc[pair, 128:256, :])
         adj[0:128, 128 * pair : 128 * pair + 128] = hi
@@ -251,10 +260,10 @@
     def rows64(p):
         return pl.ds(pl.multiple_of(p * 64, 64), 64)
 
-    def returned(p, q):
+    def returned(src, dst, key, device):
         return pltpu.make_async_remote_copy(
-            src_ref=zon.at[rows64(p)], dst_ref=back.at[rows64(q)], send_sem=send2_sem.at[p], recv_sem=recv2_sem.at[q],
-            device_id=(la, p), device_id_type=MESH,
+            src_ref=zon.at[src], dst_ref=back.at[dst], send_sem=send_sem.at[1], recv_sem=recv_sem.at[4 + key],
+            device_id=device, device_id_type=MESH,
         )
 
     for ox in (2, 1, 3, 0):
@@ -264,17 +273,15 @@
         zon[at, :] = got[:, 0:128] + got[:, 128:256] + nt(zlo[at, :], adj[0:128, :])
         for oy in (2, 1, 3, 0):
             if (ox, oy) != (0, 0):
-                returned(to_x * 4 + (y + oy) % 4, lo).start()
+                p = to_x * 4 + (y + oy) % 4
+                returned(rows64(p), rows64(lo), x, (la, p)).start()
     back[rows64(lo), :] = zon[rows64(lo), :]
-    loads[8].wait()
 
     group = lax.broadcasted_iota(I32, (64, 128), 1) >> 5
     for ox in (2, 3, 1, 0):
         f = (x + ox) % 4
-        for oy in (2, 3, 1, 0):
-            if (ox, oy) != (0, 0):
-                p = f * 4 + (y + oy) % 4
-                returned(p, p).wait_recv()
+        together = pl.ds(0, 256 if ox else 192)
+        returned(together, together, f, other).wait_recv()
         parts = [back[pl.ds(pl.multiple_of(f * 256 + 64 * s, 64), 64), :] for s in range(4)]
         rows = []
         for r in range(4):
@@ -288,31 +295,22 @@
         w = vw[at, :]
         got = nn(hi, w)
         got = got[:, 0:128] + got[:, 128:256] + nn(low, w[:, 0:128])
-        out_ref[:, at] = control[:, at] + got
-
-    def sent(step, _):
-        p = (la * 16 + lo + step) % 128
-        message(p, p, other).wait_send()
-        return 0
-
-    lax.fori_loop(1, 128, sent, 0)
-
-    def sent_back(step, _):
-        p = (lo + step) % 16
-        returned(p, p).wait_send()
-        return 0
-
-    lax.fori_loop(1, 16, sent_back, 0)
+        out_ref[:, at] = got
+
+    together = pl.ds(0, MSG * 127)
+    message(together, together, 0, other).wait_send()
+    together = pl.ds(0, 64 * 15)
+    returned(together, together, 0, other).wait_send()
 
 
 def per_device(
     control, vert_factor, zonal_factor, obs_dest, obs_cell, obs_offset, obs_count, departure, obs_rinv, obs_weights
 ):
-    anywhere = pl.BlockSpec(memory_space=pl.ANY)
+    anywhere = pl.BlockSpec(memory_space=pltpu.HBM)
     out = pl.pallas_call(
         kernel,
         out_shape=jax.ShapeDtypeStruct((256, 512), F32),
-        in_specs=[pl.BlockSpec(memory_space=pltpu.SMEM)] + [anywhere] * 9,
+        in_specs=[pl.BlockSpec(memory_space=pltpu.SMEM)] + [anywhere] * 8,
         out_specs=pl.BlockSpec(memory_space=pltpu.VMEM),
         scratch_shapes=[
             pltpu.VMEM((1, N_OBS), I32),
@@ -323,7 +321,6 @@
             pltpu.VMEM((N_OBS, 128), F32),
             pltpu.VMEM((4, 128, 128), F32),
             pltpu.VMEM((1024, 1024), F32),
-            pltpu.VMEM((256, 512), F32),
             pltpu.VMEM((N_OBS, 128), F32),
             pltpu.VMEM((272, N_OBS), BF16),
             pltpu.VMEM((SLOTS, N_OBS), BF16),
@@ -335,17 +332,13 @@
             pltpu.VMEM((512, 256), BF16),
             pltpu.VMEM((384, 128), F32),
             pltpu.VMEM((192, 128), F32),
-            pltpu.VMEM((256, 768), BF16),
-            pltpu.VMEM((128, 768), BF16),
             pltpu.VMEM((8, 256, 128), F32),
             pltpu.VMEM((256, 1024), BF16),
             pltpu.VMEM((1024, 128), F32),
             pltpu.VMEM((1024, 128), F32),
-            pltpu.SemaphoreType.DMA((128,)),
-            pltpu.SemaphoreType.DMA((128,)),
-            pltpu.SemaphoreType.DMA((16,)),
-            pltpu.SemaphoreType.DMA((16,)),
-            pltpu.SemaphoreType.DMA((9,)),
+            pltpu.SemaphoreType.DMA((2,)),
+            pltpu.SemaphoreType.DMA((8,)),
+            pltpu.SemaphoreType.DMA((8,)),
         ],
         compiler_params=pltpu.CompilerParams(
             collective_id=0, has_side_effects=True, vmem_limit_bytes=60 * 2**20
@@ -361,9 +354,8 @@
         obs_weights,
         vert_factor,
         zonal_factor,
-        control.reshape(256, 512),
     )
-    return out.reshape(4, 64, 512)
+    return control + out.reshape(4, 64, 512)
 
 
 def solution(mesh):

time: 47.5 us -> 37.6 us (0.79)
  Pallas kernels: 44.8 us -> 34.8 us
  other arithmetic: 0 us -> 1.91 us
  local copies, waits for them, and re-layouts: 1.87 us -> 0.01 us
    pallas_call x1, Pallas kernels: 44.8 us -> 34.8 us  [per_device(): pl.pallas_call(kernel, out_shape=jax.ShapeDtypeStruct((256, 512), F32), i...]
    add x0 -> x1, other arithmetic: none -> 1.91 us  [per_device(): return control + out.reshape(4, 64, 512)]
    unnamed x1 -> x2, local copies, waits for them, and re-layouts: 1.87 us -> 0.01 us
where the time goes in v3:
time: 37.6 us; the launch traced here: 37.4 us
  Pallas kernels  34.8 us (93%)
  other arithmetic  1.91 us (5%)
  between operations  0.73 us (2%)
    pallas_call x1, Pallas kernels, per_device(): pl.pallas_call(kernel, out_shape=jax.ShapeDtypeStruct((256, 512), F32), i...  34.8 us
    add x1, other arithmetic, per_device(): return control + out.reshape(4, 64, 512)  1.91 us

profile of v3, /device:TPU:1, one launch (start us, length us, event | category | flops | bytes accessed | tf_op | source)
XLA Modules:
  0.0 37.4 jit_solution(428643754482701342)
XLA Ops:
  0.0 0.0 copy-start
  0.7 34.8 %gradient.1 = f32[256,512]{1,0:T(8,128)} custom-call(s32[1]{0:T(128)S(6)} %copy.11.count_ref, s32[1,768]{1,0:T(1,128)} %bitcast.3, s32[768]{0:T(1024)} %cell_hbm.1, s32[768]{0:T(1024)} %off_hbm.1, f32[768]{0:T(1024)} %dep_hbm.1, f32[768]{0:T(1024)} %rinv_hbm.1, f32[768,128]{1,0:T(8,128)} %w_hbm.1, f32[4,128,128]{2,1,0:T(8,128)} %vert_hbm.1, f32[1024,1024]{1,0:T(8,128)} %z_hbm.1), custom_call_target="tpu_custom_call" | custom-call | tf_op jit(solution)/shard_map/gradient/pallas_call | solution.py:310
  35.5 0.0 copy-done
  35.5 1.9 %add.3 = f32[4,64,512]{2,1,0:T(8,128)} add(f32[4,64,512]{2,1,0:T(8,128)S(1)} %copy-done, f32[4,64,512]{2,1,0:T(8,128)} %bitcast.2) | non-fusion elementwise | flops 131072 | bytes 1572864 | tf_op jit(solution)/shard_map/add | solution.py:358
Async XLA Ops:
  0.0 35.5 %copy-start = (f32[4,64,512]{2,1,0:T(8,128)S(1)}, f32[4,64,512]{2,1,0:T(8,128)}, u32[]{:S(2)}) copy-start(f32[4,64,512]{2,1,0:T(8,128)} %param.10) | copy-start | bytes 1572868

commit v4 on v3

--- a/solution.py
+++ b/solution.py
@@ -21,9 +21,13 @@
     return min(o, 4 - o)
 
 
+def hops(o):
+    return ring(o[0]) + ring(o[2]) + ring(o[3])
+
+
 def offsets():
     found = [(z, c, x, y) for z in range(4) for c in range(2) for x in range(4) for y in range(4)][1:]
-    return sorted(found, key=lambda o: ((o[0] + o[2] + o[3]) % 4, -(ring(o[0]) + ring(o[2]) + ring(o[3]))))
+    return sorted(found, key=lambda o: ((o[0] + o[2] + o[3]) % 4, -hops(o)))
 
 
 ALL = offsets()
@@ -200,7 +204,7 @@
     la, lo = lax.axis_index("lat"), lax.axis_index("lon")
     z, x, y = la // 2, lo // 4, lo % 4
     barrier = pltpu.get_barrier_semaphore()
-    for o in ALL:
+    for o in sorted(ALL, key=hops, reverse=True):
         pl.semaphore_signal(barrier, inc=1, device_id=peer(la, lo, o), device_id_type=MESH)
     loads = [
         pltpu.make_async_copy(src, dst, load_sem.at[n])
@@ -309,7 +313,7 @@
     anywhere = pl.BlockSpec(memory_space=pltpu.HBM)
     out = pl.pallas_call(
         kernel,
-        out_shape=jax.ShapeDtypeStruct((256, 512), F32),
+        out_shape=pltpu.VMEM((256, 512), F32),
         in_specs=[pl.BlockSpec(memory_space=pltpu.SMEM)] + [anywhere] * 8,
         out_specs=pl.BlockSpec(memory_space=pltpu.VMEM),
         scratch_shapes=[
@@ -341,19 +345,18 @@
             pltpu.SemaphoreType.DMA((8,)),
         ],
         compiler_params=pltpu.CompilerParams(
-            collective_id=0, has_side_effects=True, vmem_limit_bytes=60 * 2**20
+            collective_id=0, has_side_effects=True, vmem_limit_bytes=40 * 2**20
         ),
         name="gradient",
     )(
         obs_count,
-        obs_dest.reshape(1, N_OBS),
-        obs_cell,
-        obs_offset,
-        departure,
-        obs_rinv,
-        obs_weights,
-        vert_factor,
-        zonal_factor,
+        *(
+            pltpu.with_memory_space_constraint(x, pltpu.HBM)
+            for x in (
+                obs_dest.reshape(1, N_OBS), obs_cell, obs_offset, departure, obs_rinv, obs_weights,
+                vert_factor, zonal_factor,
+            )
+        )
     )
     return control + out.reshape(4, 64, 512)
 

time: 37.6 us -> 35.2 us (0.936)
  Pallas kernels: 34.8 us -> 33.5 us
  other arithmetic: 1.91 us -> 0.87 us
    pallas_call x1, Pallas kernels: 34.8 us -> 33.5 us  [per_device(): pl.pallas_call(kernel, out_shape=pltpu.VMEM((256, 512), F32), in_specs=[p...]
    add x1, other arithmetic: 1.91 us -> 0.87 us  [per_device(): return control + out.reshape(4, 64, 512)]
where the time goes in v4:
time: 35.2 us; the launch traced here: 35.1 us
  Pallas kernels  33.5 us (95%)
  other arithmetic  0.87 us (2%)
  between operations  0.73 us (2%)
    pallas_call x1, Pallas kernels, per_device(): pl.pallas_call(kernel, out_shape=pltpu.VMEM((256, 512), F32), in_specs=[p...  33.5 us
    add x1, other arithmetic, per_device(): return control + out.reshape(4, 64, 512)  0.87 us

profile of v4, /device:TPU:1, one launch (start us, length us, event | category | flops | bytes accessed | tf_op | source)
XLA Modules:
  0.0 35.1 jit_solution(6180132902629053806)
XLA Ops:
  0.0 0.0 copy-start
  0.7 33.5 %gradient.1 = f32[256,512]{1,0:T(8,128)S(1)} custom-call(s32[1]{0:T(128)S(6)} %copy.11.count_ref, s32[1,768]{1,0:T(1,128)} %bitcast.3, s32[768]{0:T(1024)} %cell_hbm.1, s32[768]{0:T(1024)} %off_hbm.1, f32[768]{0:T(1024)} %dep_hbm.1, f32[768]{0:T(1024)} %rinv_hbm.1, f32[768,128]{1,0:T(8,128)} %w_hbm.1, f32[4,128,128]{2,1,0:T(8,128)} %vert_hbm.1, ...), custom_call_target="tpu_custom_call" | custom-call | tf_op jit(solution)/shard_map/gradient/pallas_call | solution.py:314
  34.2 0.0 copy-done
  34.2 0.9 %add.3 = f32[4,64,512]{2,1,0:T(8,128)} add(f32[4,64,512]{2,1,0:T(8,128)S(1)} %copy-done, f32[4,64,512]{2,1,0:T(8,128)S(1)} %bitcast.2) | non-fusion elementwise | flops 131072 | bytes 1572864 | tf_op jit(solution)/shard_map/add | solution.py:361
Async XLA Ops:
  0.0 34.2 %copy-start = (f32[4,64,512]{2,1,0:T(8,128)S(1)}, f32[4,64,512]{2,1,0:T(8,128)}, u32[]{:S(2)}) copy-start(f32[4,64,512]{2,1,0:T(8,128)} %param.10) | copy-start | bytes 1572868

commit v5 on v4

--- a/solution.py
+++ b/solution.py
@@ -27,7 +27,7 @@
 
 def offsets():
     found = [(z, c, x, y) for z in range(4) for c in range(2) for x in range(4) for y in range(4)][1:]
-    return sorted(found, key=lambda o: ((o[0] + o[2] + o[3]) % 4, -hops(o)))
+    return sorted(found, key=lambda o: ((2, 1, 3, 0).index((o[0] + o[2] + o[3]) % 4), -hops(o)))
 
 
 ALL = offsets()
@@ -204,8 +204,6 @@
     la, lo = lax.axis_index("lat"), lax.axis_index("lon")
     z, x, y = la // 2, lo // 4, lo % 4
     barrier = pltpu.get_barrier_semaphore()
-    for o in sorted(ALL, key=hops, reverse=True):
-        pl.semaphore_signal(barrier, inc=1, device_id=peer(la, lo, o), device_id_type=MESH)
     loads = [
         pltpu.make_async_copy(src, dst, load_sem.at[n])
         for n, (src, dst) in enumerate(
@@ -215,7 +213,11 @@
             )
         )
     ]
-    for load in loads:
+    for load in loads[:6]:
+        load.start()
+    for o in sorted(ALL, key=hops, reverse=True):
+        pl.semaphore_signal(barrier, inc=1, device_id=peer(la, lo, o), device_id_type=MESH)
+    for load in loads[6:]:
         load.start()
     for load in loads[:6]:
         load.wait()
@@ -251,11 +253,11 @@
     factors(vert_ref, zf, zhi, zlo, vw)
     acc[...] = jnp.zeros_like(acc)
 
-    for k in range(4):
+    for k in (2, 1, 3, 0):
         key = (my_key + 4 - k) % 4
         together = pl.ds(0, MSG * (32 if k else 31))
         message(together, together, key, other).wait_recv()
-        scatter(lo % 4, pl.multiple_of(key * 512, 512), k == 3, recv, tv, tm, acc)
+        scatter(lo % 4, pl.multiple_of(key * 512, 512), k == 0, recv, tv, tm, acc)
     for pair in range(8):
         hi, low = split(acc[pair, 0:128, :] + acc[pair, 128:256, :])
         adj[0:128, 128 * pair : 128 * pair + 128] = hi

time: 35.2 us -> 34.8 us (0.989)
  Pallas kernels: 33.5 us -> 33.1 us
    pallas_call x1, Pallas kernels: 33.5 us -> 33.1 us  [per_device(): pl.pallas_call(kernel, out_shape=pltpu.VMEM((256, 512), F32), in_specs=[p...]
where the time goes in v5:
time: 34.8 us; the launch traced here: 34.7 us
  Pallas kernels  33.1 us (95%)
  other arithmetic  0.87 us (2%)
  between operations  0.73 us (2%)
    pallas_call x1, Pallas kernels, per_device(): pl.pallas_call(kernel, out_shape=pltpu.VMEM((256, 512), F32), in_specs=[p...  33.1 us
    add x1, other arithmetic, per_device(): return control + out.reshape(4, 64, 512)  0.87 us

profile of v5, /device:TPU:1, one launch (start us, length us, event | category | flops | bytes accessed | tf_op | source)
XLA Modules:
  0.0 34.7 jit_solution(10331616976219983847)
XLA Ops:
  0.0 0.0 copy-start
  0.7 33.1 %gradient.1 = f32[256,512]{1,0:T(8,128)S(1)} custom-call(s32[1]{0:T(128)S(6)} %copy.11.count_ref, s32[1,768]{1,0:T(1,128)} %bitcast.3, s32[768]{0:T(1024)} %cell_hbm.1, s32[768]{0:T(1024)} %off_hbm.1, f32[768]{0:T(1024)} %dep_hbm.1, f32[768]{0:T(1024)} %rinv_hbm.1, f32[768,128]{1,0:T(8,128)} %w_hbm.1, f32[4,128,128]{2,1,0:T(8,128)} %vert_hbm.1, ...), custom_call_target="tpu_custom_call" | custom-call | tf_op jit(solution)/shard_map/gradient/pallas_call | solution.py:316
  33.8 0.0 copy-done
  33.8 0.9 %add.3 = f32[4,64,512]{2,1,0:T(8,128)} add(f32[4,64,512]{2,1,0:T(8,128)S(1)} %copy-done, f32[4,64,512]{2,1,0:T(8,128)S(1)} %bitcast.2) | non-fusion elementwise | flops 131072 | bytes 1572864 | tf_op jit(solution)/shard_map/add | solution.py:363
Async XLA Ops:
  0.0 33.8 %copy-start = (f32[4,64,512]{2,1,0:T(8,128)S(1)}, f32[4,64,512]{2,1,0:T(8,128)}, u32[]{:S(2)}) copy-start(f32[4,64,512]{2,1,0:T(8,128)} %param.10) | copy-start | bytes 1572868
